TPU v7x, 32 devices: a whole 2x2x4 slice. The times are simulated.
32 devices in a mesh: seq: 8 (over z, core), fsdp: 4 (over y, x).
Axes of the slice: x: 2, y: 2, z: 4, core: 2. Of those that a mesh axis runs over, the one named last changes fastest.
Arguments:
- tokens: bfloat16 [4, 1024, 1024], P('fsdp', 'seq'), may hold values from -6 to 6
- ln1_gain: float32 [1024], replicated, may hold values from 0.25 to 1.75
- ln1_bias: float32 [1024], replicated, may hold values from -3 to 3
- qkv_weight: bfloat16 [1024, 3072], P(('seq', 'fsdp')), may hold values from -0.1875 to 0.1875
- qkv_bias: float32 [3072], replicated, may hold values from -2.5 to 2.5
- out_weight: bfloat16 [1024, 1024], P(('seq', 'fsdp')), may hold values from -3 to 3
- ln2_gain: float32 [1024], replicated, may hold values from 0.25 to 1.75
- ln2_bias: float32 [1024], replicated, may hold values from -3 to 3
- gate_up_weight: bfloat16 [1024, 5632], P(('seq', 'fsdp')), may hold values from -0.1875 to 0.1875
- down_weight: bfloat16 [2816, 1024], P(('seq', 'fsdp')), may hold values from -0.109375 to 0.109375
- out_grad: bfloat16 [4, 1024, 1024], P('fsdp', 'seq'), may hold values from -6 to 6
Outputs:
- block_out: bfloat16 [4, 1024, 1024], P('fsdp', 'seq')
- input_grad: float32 [4, 1024, 1024], P('fsdp', 'seq')
- ln1_gain_grad: float32 [1024], replicated
- ln1_bias_grad: float32 [1024], replicated
- qkv_weight_grad: float32 [1024, 3072], P(('seq', 'fsdp'))
- qkv_bias_grad: float32 [3072], replicated
- out_weight_grad: float32 [1024, 1024], P(('seq', 'fsdp'))
- ln2_gain_grad: float32 [1024], replicated
- ln2_bias_grad: float32 [1024], replicated
- gate_up_weight_grad: float32 [1024, 5632], P(('seq', 'fsdp'))
- down_weight_grad: float32 [2816, 1024], P(('seq', 'fsdp'))
All inputs are finite; a program needn't handle non-finite values.
Results may differ from a plain program's by a relative error of at most 0.011.
Values may be sent and summed in bfloat16 or wider, within the bound.
No kernel may reach another device: no remote copies, remote signals or barrier semaphores. Data moves between devices by JAX's collectives and lax.ppermute only.
A program may use at most 192 MiB of HBM per device.

v0:
```python
import jax
import jax.numpy as jnp
from jax import lax
from jax.sharding import PartitionSpec as P

H = 16
HD = 64
ROT = 16
EPS = 1e-05


def layer_norm(values, gain_vec, shift_vec):
    average = jnp.mean(values, axis=-1, keepdims=True)
    centred = values - average
    variance = jnp.mean(centred * centred, axis=-1, keepdims=True)
    return centred * lax.rsqrt(variance + EPS) * gain_vec + shift_vec


def rotary_tables(positions):
    half_rot = ROT // 2
    frequency = 10000.0 ** (-2.0 * jnp.arange(half_rot).astype(jnp.float32) / ROT)
    angles = positions.astype(jnp.float32)[:, None] * frequency[None, :]
    return (jnp.cos(angles)[:, None, :], jnp.sin(angles)[:, None, :])


def rotate(heads_in, positions):
    half_rot = ROT // 2
    cosines, sines = rotary_tables(positions)
    lower_half = heads_in[..., :half_rot]
    upper_half = heads_in[..., half_rot:ROT]
    return jnp.concatenate(
        [
            lower_half * cosines - upper_half * sines,
            upper_half * cosines + lower_half * sines,
            heads_in[..., ROT:],
        ],
        axis=-1,
    )


def unrotate(grads_in, positions):
    half_rot = ROT // 2
    cosines, sines = rotary_tables(positions)
    lower_half = grads_in[..., :half_rot]
    upper_half = grads_in[..., half_rot:ROT]
    return jnp.concatenate(
        [
            lower_half * cosines + upper_half * sines,
            upper_half * cosines - lower_half * sines,
            grads_in[..., ROT:],
        ],
        axis=-1,
    )


def swiglu(gate_up):
    half_width = gate_up.shape[-1] // 2
    return jax.nn.silu(gate_up[:, :half_width]) * gate_up[:, half_width:]


def contract_last(left, right):
    return lax.dot_general(
        left, right, (((1,), (1,)), ((), ())), preferred_element_type=jnp.float32
    )


def column_term(left, right):
    return lax.dot_general(
        left, right, (((0,), (0,)), ((), ())), preferred_element_type=jnp.float32
    )


def attend(queries, keys_in, values_in):
    length = queries.shape[0]
    block_rows = min(512, length)
    scaling = queries.shape[2] ** (-0.5)
    key_index = jnp.arange(length, dtype=jnp.int32)

    def one_block(args):
        query_block, first_row = args
        scores = (
            jnp.einsum("qhd,khd->hqk", query_block, keys_in, preferred_element_type=jnp.float32)
            * scaling
        )
        causal = (first_row + jnp.arange(block_rows, dtype=jnp.int32))[:, None] >= key_index[
            None, :
        ]
        scores = jnp.where(causal[None], scores, -jnp.inf)
        row_max = jnp.max(scores, axis=-1, keepdims=True)
        exponent = jnp.exp(scores - row_max)
        normaliser = jnp.sum(exponent, axis=-1, keepdims=True)
        weights = (exponent / normaliser).astype(jnp.bfloat16)
        out_block = jnp.einsum(
            "hqk,khd->qhd", weights, values_in, preferred_element_type=jnp.float32
        )
        return (out_block, (row_max + jnp.log(normaliser))[..., 0])

    blocks = queries.reshape(length // block_rows, block_rows, queries.shape[1], queries.shape[2])
    starts = jnp.arange(length // block_rows, dtype=jnp.int32) * block_rows
    out_blocks, totals = lax.map(one_block, (blocks, starts))
    return (out_blocks.reshape(queries.shape), totals)


def attend_back(queries, keys_in, values_in, log_total, grad_out):
    length = queries.shape[0]
    block_rows = min(512, length)
    scaling = queries.shape[2] ** (-0.5)
    key_index = jnp.arange(length, dtype=jnp.int32)

    def one_block(carry, args):
        grad_keys, grad_values = carry
        query_block, grad_block, total_block, first_row = args
        scores = (
            jnp.einsum("qhd,khd->hqk", query_block, keys_in, preferred_element_type=jnp.float32)
            * scaling
        )
        causal = (first_row + jnp.arange(block_rows, dtype=jnp.int32))[:, None] >= key_index[
            None, :
        ]
        scores = jnp.where(causal[None], scores, -jnp.inf)
        probs = jnp.exp(scores - total_block[..., None])
        grad_probs = jnp.einsum(
            "qhd,khd->hqk", grad_block, values_in, preferred_element_type=jnp.float32
        )
        row_dot = jnp.sum(probs * grad_probs, axis=-1, keepdims=True)
        grad_scores = (probs * (grad_probs - row_dot)).astype(jnp.bfloat16)
        grad_query = (
            jnp.einsum("hqk,khd->qhd", grad_scores, keys_in, preferred_element_type=jnp.float32)
            * scaling
        )
        grad_keys = (
            grad_keys
            + jnp.einsum(
                "hqk,qhd->khd", grad_scores, query_block, preferred_element_type=jnp.float32
            )
            * scaling
        )
        grad_values = grad_values + jnp.einsum(
            "hqk,qhd->khd",
            probs.astype(jnp.bfloat16),
            grad_block,
            preferred_element_type=jnp.float32,
        )
        return ((grad_keys, grad_values), grad_query)

    block_shape = (length // block_rows, block_rows, queries.shape[1], queries.shape[2])
    starts = jnp.arange(length // block_rows, dtype=jnp.int32) * block_rows
    zeros = jnp.zeros(keys_in.shape, jnp.float32)
    (grad_keys, grad_values), grad_queries = lax.scan(
        one_block,
        (zeros, zeros),
        (queries.reshape(block_shape), grad_out.reshape(block_shape), log_total, starts),
    )
    return (grad_queries.reshape(queries.shape), grad_keys, grad_values)


def on_device(
    tokens,
    ln1_gain,
    ln1_bias,
    qkv_weight,
    qkv_bias,
    out_weight,
    ln2_gain,
    ln2_bias,
    gate_up_weight,
    down_weight,
    out_grad,
):
    tok_rows = tokens.shape[1]
    width = tokens.shape[2]
    residual = tokens.reshape(tok_rows, width).astype(jnp.float32)
    cotangent = out_grad.reshape(tok_rows, width)
    qkv_full, proj_full = (
        lax.all_gather(qkv_weight, ("seq", "fsdp"), axis=0, tiled=True),
        lax.all_gather(out_weight, ("seq", "fsdp"), axis=0, tiled=True),
    )
    normed1, ln1_pull = jax.vjp(layer_norm, residual, ln1_gain, ln1_bias)
    hidden1 = normed1.astype(jnp.bfloat16)
    projected = jnp.dot(hidden1, qkv_full, preferred_element_type=jnp.float32) + qkv_bias
    projected = projected.reshape(tok_rows, 3, H, HD)
    positions = lax.axis_index("seq") * tok_rows + jnp.arange(tok_rows, dtype=jnp.int32)
    packed = jnp.stack(
        [rotate(projected[:, 0], positions), rotate(projected[:, 1], positions), projected[:, 2]],
        axis=1,
    )
    packed = packed.reshape(tok_rows, 3, width).astype(jnp.bfloat16)
    by_heads = lax.all_to_all(packed, "seq", split_axis=2, concat_axis=0, tiled=True)
    length = by_heads.shape[0]
    local_heads = by_heads.shape[2] // HD
    queries = by_heads[:, 0].reshape(length, local_heads, HD)
    keys_in = by_heads[:, 1].reshape(length, local_heads, HD)
    values_in = by_heads[:, 2].reshape(length, local_heads, HD)
    attended, log_total = attend(queries, keys_in, values_in)
    attended_b = attended.reshape(length, local_heads * HD).astype(jnp.bfloat16)
    gathered_out = lax.all_to_all(attended_b, "seq", split_axis=0, concat_axis=1, tiled=True)
    middle = residual + jnp.dot(gathered_out, proj_full, preferred_element_type=jnp.float32)
    gate_up_full, down_full = (
        lax.all_gather(gate_up_weight, ("seq", "fsdp"), axis=0, tiled=True),
        lax.all_gather(down_weight, ("seq", "fsdp"), axis=0, tiled=True),
    )
    normed2, ln2_pull = jax.vjp(layer_norm, middle, ln2_gain, ln2_bias)
    hidden2 = normed2.astype(jnp.bfloat16)
    gate_up = jnp.dot(hidden2, gate_up_full, preferred_element_type=jnp.float32)
    activation, swiglu_pull = jax.vjp(swiglu, gate_up)
    activation_b = activation.astype(jnp.bfloat16)
    block_out = (
        middle + jnp.dot(activation_b, down_full, preferred_element_type=jnp.float32)
    ).astype(jnp.bfloat16)
    gate_up_back, down_back = (
        lax.all_gather(gate_up_weight, ("seq", "fsdp"), axis=0, tiled=True),
        lax.all_gather(down_weight, ("seq", "fsdp"), axis=0, tiled=True),
    )
    grad_act = contract_last(cotangent, down_back)
    down_grad = lax.psum_scatter(
        column_term(activation_b, cotangent), ("seq", "fsdp"), scatter_dimension=0, tiled=True
    )
    (grad_gate_up,) = swiglu_pull(grad_act)
    grad_gate_up_b = grad_gate_up.astype(jnp.bfloat16)
    gate_up_grad = lax.psum_scatter(
        column_term(hidden2, grad_gate_up_b), ("seq", "fsdp"), scatter_dimension=0, tiled=True
    )
    grad_hidden2 = contract_last(grad_gate_up_b, gate_up_back)
    grad_middle, ln2_gain_part, ln2_bias_part = ln2_pull(grad_hidden2)
    grad_middle = grad_middle + cotangent.astype(jnp.float32)
    grad_middle_b = grad_middle.astype(jnp.bfloat16)
    qkv_back, proj_back = (
        lax.all_gather(qkv_weight, ("seq", "fsdp"), axis=0, tiled=True),
        lax.all_gather(out_weight, ("seq", "fsdp"), axis=0, tiled=True),
    )
    out_weight_grad = lax.psum_scatter(
        column_term(gathered_out, grad_middle_b), ("seq", "fsdp"), scatter_dimension=0, tiled=True
    )
    grad_out_tok = contract_last(grad_middle_b, proj_back).astype(jnp.bfloat16)
    grad_heads = lax.all_to_all(grad_out_tok, "seq", split_axis=1, concat_axis=0, tiled=True)
    grad_query, grad_key, grad_value = attend_back(
        queries, keys_in, values_in, log_total, grad_heads.reshape(length, local_heads, HD)
    )
    head_positions = jnp.arange(length, dtype=jnp.int32)
    grad_packed = jnp.stack(
        [unrotate(grad_query, head_positions), unrotate(grad_key, head_positions), grad_value],
        axis=1,
    )
    grad_packed = grad_packed.reshape(length, 3, local_heads * HD).astype(jnp.bfloat16)
    grad_tokens = lax.all_to_all(grad_packed, "seq", split_axis=0, concat_axis=2, tiled=True)
    grad_projected = grad_tokens.reshape(tok_rows, 3 * width)
    qkv_weight_grad = lax.psum_scatter(
        column_term(hidden1, grad_projected), ("seq", "fsdp"), scatter_dimension=0, tiled=True
    )
    grad_hidden1 = contract_last(grad_projected, qkv_back)
    bias_part = jnp.sum(grad_projected.astype(jnp.float32), axis=0)
    grad_input, ln1_gain_part, ln1_bias_part = ln1_pull(grad_hidden1)
    grad_input = grad_input + grad_middle
    summed = lax.psum(
        (ln1_gain_part, ln1_bias_part, bias_part, ln2_gain_part, ln2_bias_part), ("seq", "fsdp")
    )
    return (
        block_out.reshape(1, tok_rows, width),
        grad_input.reshape(1, tok_rows, width),
        summed[0],
        summed[1],
        qkv_weight_grad,
        summed[2],
        out_weight_grad,
        summed[3],
        summed[4],
        gate_up_grad,
        down_grad,
    )


def solution(mesh):
    placed = (
        P("fsdp", "seq", None),
        P(),
        P(),
        P(("seq", "fsdp"), None),
        P(),
        P(("seq", "fsdp"), None),
        P(),
        P(),
        P(("seq", "fsdp"), None),
        P(("seq", "fsdp"), None),
        P("fsdp", "seq", None),
    )
    return jax.shard_map(
        on_device,
        mesh=mesh,
        in_specs=placed,
        out_specs=(
            P("fsdp", "seq", None),
            P("fsdp", "seq", None),
            P(),
            P(),
            P(("seq", "fsdp"), None),
            P(),
            P(("seq", "fsdp"), None),
            P(),
            P(),
            P(("seq", "fsdp"), None),
            P(("seq", "fsdp"), None),
        ),
        check_vma=False,
    )
```

profile of v0, /device:TPU:0, one launch (start us, length us, event | category | flops | bytes accessed | tf_op | source)
XLA Modules:
  0.0 1387.9 jit_solution(4007856806318512705)
XLA Ops:
  12.9 70.3 %all-gather.5.cloned.1.call-done = bf16[1024,3072]{1,0:T(8,128)(2,1)} async-done(((bf16[32,3072]{1,0:T(8,128)(2,1)}), bf16[1024,3072]{1,0:T(8,128)(2,1)}) %all-gather.5.cloned.1.call-update) | async-done | bytes 6291472 | tf_op jit(solution)/shard_map/all_gather | solution.py:175
  83.2 3.9 convolution_add_fusion
  88.0 1.7 copy.58
  89.7 3.6 all-to-all-start
  93.3 30.2 %all-to-all-done = bf16[128,3,1024]{0,1,2:T(4,128)(2,1)S(1)} async-done(((bf16[128,3,1024]{0,1,2:T(4,128)(2,1)}), bf16[128,3,1024]{0,1,2:T(4,128)(2,1)S(1)}, u32[]{:S(2)}, u32[]{:S(2)}) %all-to-all-start) | async-done | bytes 786464 | tf_op jit(solution)/shard_map/all_to_all | solution.py:188
  126.1 14.4 %while.28 = (s32[]{:T(128)}, bf16[2,512,2,64]{1,3,2,0:T(8,128)(2,1)S(1)}, f32[2,2,512]{2,1,0:T(2,128)S(1)}, s32[2]{0:T(128)S(1)}, bf16[2,512,2,64]{1,3,2,0:T(8,1...) while((s32[]{:T(128)}, ...), condition=%wide.region_5.6_spmd.clone, body=%wide.region_2.5_spmd.clone.sunk | while | flops 281542144 | bytes 15634553 | solution.py:100
  127.7 2.0 fusion.139
  130.8 2.4 fusion.141
  134.9 2.0 fusion.139
  138.1 2.4 fusion.141
  141.8 3.6 all-to-all-start.1
  145.4 9.4 all-to-all-done.1
  154.9 2.2 fusion.94
  157.3 79.5 %all-gather.9.cloned.1.call-done = bf16[1024,5632]{1,0:T(8,128)(2,1)} async-done(((bf16[32,5632]{1,0:T(8,128)(2,1)}), bf16[1024,5632]{1,0:T(8,128)(2,1)}) %all-gather.9.cloned.1.call-update) | async-done | bytes 11534352 | tf_op jit(solution)/shard_map/all_gather | solution.py:199
  236.8 7.7 fusion.90
  244.5 60.7 %all-gather.11.cloned.1.call-done = bf16[2816,1024]{1,0:T(8,128)(2,1)} async-done(((bf16[88,1024]{1,0:T(8,128)(2,1)}), bf16[2816,1024]{1,0:T(8,128)(2,1)}) %all-gather.11.cloned.1.call-update) | async-done | bytes 5767184 | tf_op jit(solution)/shard_map/all_gather | solution.py:200
  305.2 7.7 fusion.84
  313.0 6.6 multiply_reduce_fusion.1
  319.5 1.3 fusion.92
  322.7 1.5 convolution_convert_fusion
  324.3 1.8 copy.71
  326.1 3.6 all-to-all-start.2
  329.7 3.6 fusion.95
  333.8 5.6 all-to-all-done.2
  340.4 42.1 %while.29 = (s32[]{:T(128)}, f32[1024,2,64]{0,2,1:T(8,128)}, f32[1024,2,64]{0,2,1:T(8,128)}, f32[2,512,2,64]{1,0,3,2:T(2,128)}, bf16[2,512,2,64]{1,3,2,0:T(8,128...) while((s32[]{:T(128)}, f32[1024,2,64]{0,2,1:T(8,128)}, ...), condition=%wide.region_12.13_spmd.clone, body=%wide.region_10.12_spmd.clone.sunk | while | flops 688061952 | bytes 55083208 | solution.py:149
  340.4 1.6 fusion.151
  343.8 2.8 multiply_reduce_fusion.5
  346.6 1.3 multiply_convert_fusion.3
  347.9 2.2 fusion.152
  350.1 4.4 fusion.153
  355.6 5.7 dynamic_update_slice.21
  361.3 1.6 fusion.151
  364.7 2.8 multiply_reduce_fusion.5
  367.5 1.3 multiply_convert_fusion.3
  368.8 2.4 fusion.152
  371.2 4.5 fusion.153
  376.8 5.7 dynamic_update_slice.21
  384.7 1.5 reshape.364
  388.0 33.2 %all_to_all.65 = bf16[1024,3,128]{2,1,0:T(4,128)(2,1)S(1)} all-to-all(bf16[1024,3,128]{2,1,0:T(4,128)(2,1)S(1)} %copy.68), channel_id=1, replica_groups=mesh['seq'=8,'fsdp'=4] {'seq'}, dimensions={0} | all-to-all | bytes 1572864 | tf_op jit(solution)/shard_map/all_to_all | solution.py:245
  421.9 6.5 fusion.67
  429.6 5.9 fusion.70
  436.8 10.9 fusion.82
  448.8 4.3 fusion.48
  453.1 5.1 fusion.91
  458.6 38.4 %all-reduce.2 = (f32[1024]{0:T(1024)}, f32[1024]{0:T(1024)}, f32[3072]{0:T(1024)}, f32[1024]{0:T(1024)}, f32[1024]{0:T(1024)}) all-reduce(f32[1024]{0:T(1024)S(1)} %get-tuple-element.239, f32[1024]{0:T(1024)S(1)} %get-tuple-element.242, f32[3072]{0:T(1024)S(1)} %bitcast.210, ...), channel_id=1, replica_groups=mesh['seq'=8,'fsdp'=4] {'seq','fsdp'}, use_global_device_ids=true, to_apply=%region_16.17 | all-reduce | flops 7168 | bytes 57344 | tf_op jit(solution)/shard_map/psum | solution.py:254
  498.1 138.9 %reduce-scatter.5.cloned.1.call-done = f32[32,3072]{1,0:T(8,128)} async-done(((f32[1024,3072]{1,0:T(8,128)}), f32[32,3072]{1,0:T(8,128)}) %reduce-scatter.5.cloned.1.call-update) | async-done | bytes 393232 | tf_op jit(solution)/shard_map/reduce_scatter | solution.py:247
  637.1 250.8 %reduce-scatter.11.cloned.1.call-done = f32[88,1024]{1,0:T(8,128)} async-done(((f32[2816,1024]{1,0:T(8,128)}), f32[88,1024]{1,0:T(8,128)}) %reduce-scatter.11.cloned.1.call-update) | async-done | bytes 360464 | tf_op jit(solution)/shard_map/reduce_scatter | solution.py:215
  887.9 493.1 %reduce-scatter.9.cloned.1.call-done = f32[32,5632]{1,0:T(8,128)} async-done(((f32[1024,5632]{1,0:T(8,128)}), f32[32,5632]{1,0:T(8,128)}) %reduce-scatter.9.cloned.1.call-update) | async-done | bytes 720912 | tf_op jit(solution)/shard_map/reduce_scatter | solution.py:220
  (134 shorter events, 34.6 us)
Async XLA Ops:
  7.2 76.0 %all-gather.5.cloned.1.call-start = ((), (), s32[]{:S(2)}) async-start(), calls=%async_computation.8 | async-start | bytes 6488064 | tf_op jit(solution)/shard_map/all_gather | solution.py:175
  7.9 137.5 %all-gather.7.cloned.1.call-start = ((), (), s32[]{:S(2)}) async-start(), calls=%async_computation.9 | async-start | bytes 2162688 | tf_op jit(solution)/shard_map/all_gather | solution.py:176
  8.7 228.1 %all-gather.9.cloned.1.call-start = ((), (), s32[]{:S(2)}) async-start(), calls=%async_computation.10 | async-start | bytes 11894784 | tf_op jit(solution)/shard_map/all_gather | solution.py:199
  9.4 295.8 %all-gather.11.cloned.1.call-start = ((), (), s32[]{:S(2)}) async-start(), calls=%async_computation.11 | async-start | bytes 5947392 | tf_op jit(solution)/shard_map/all_gather | solution.py:200
  12.2 0.5 copy-start.17
  89.7 33.8 %all-to-all-start = ((bf16[128,3,1024]{0,1,2:T(4,128)(2,1)}), bf16[128,3,1024]{0,1,2:T(4,128)(2,1)S(1)}, u32[]{:S(2)}, u32[]{:S(2)}) async-start(bf16[128,3,1024]{0,1,2:T(4,128)(2,1)} %copy.58), calls=%async_computation | async-start | bytes 2097152 | tf_op jit(solution)/shard_map/all_to_all | solution.py:188
  126.1 28.7 %copy-start.2 = (bf16[1,128,1024]{2,1,0:T(8,128)(2,1)S(1)}, bf16[1,128,1024]{2,1,0:T(8,128)(2,1)}, u32[]{:S(2)}) copy-start(bf16[1,128,1024]{2,1,0:T(8,128)(2,1)} %param.15) | copy-start | bytes 786436
  140.5 96.3 %copy-start.13 = (f32[1024]{0:T(1024)S(1)}, f32[1024]{0:T(1024)}, u32[]{:S(2)}) copy-start(f32[1024]{0:T(1024)} %param.21) | copy-start | bytes 12292
  140.6 96.3 %copy-start.15 = (f32[1024]{0:T(1024)S(1)}, f32[1024]{0:T(1024)}, u32[]{:S(2)}) copy-start(f32[1024]{0:T(1024)} %param.22) | copy-start | bytes 12292
  141.8 13.1 all-to-all-start.1
  154.8 2.5 copy-start.12
  157.3 147.9 %copy-start.10 = (bf16[1,128,1024]{2,1,0:T(8,128)(2,1)S(1)}, bf16[1,128,1024]{2,1,0:T(8,128)(2,1)}, u32[]{:S(2)}) copy-start(bf16[1,128,1024]{2,1,0:T(8,128)(2,1)} %param.25) | copy-start | bytes 786436
  305.2 7.7 copy-start.1
  313.0 9.8 copy-start.4
  320.8 0.8 copy-start.6
  326.1 13.3 all-to-all-start.2
  329.6 168.5 %reduce-scatter.7.cloned.1.call-start = ((), (), s32[]{:S(2)}) async-start(), calls=%async_computation.13 | async-start | bytes 4325376 | tf_op jit(solution)/shard_map/reduce_scatter | solution.py:231
  333.3 303.8 %reduce-scatter.5.cloned.1.call-start = ((), (), s32[]{:S(2)}) async-start(), calls=%async_computation.12 | async-start | bytes 12976128 | tf_op jit(solution)/shard_map/reduce_scatter | solution.py:247
  342.1 4.5 copy-start
  362.9 4.5 copy-start
  387.2 34.7 %copy-start.3 = (bf16[1,128,1024]{2,1,0:T(8,128)(2,1)S(1)}, bf16[1,128,1024]{2,1,0:T(8,128)(2,1)}, u32[]{:S(2)}) copy-start(bf16[1,128,1024]{2,1,0:T(8,128)(2,1)} %param.15) | copy-start | bytes 786436
  387.2 34.7 %copy-start.14 = (f32[1024]{0:T(1024)S(1)}, f32[1024]{0:T(1024)}, u32[]{:S(2)}) copy-start(f32[1024]{0:T(1024)} %param.16) | copy-start | bytes 12292
  387.2 34.7 %copy-start.16 = (f32[1024]{0:T(1024)S(1)}, f32[1024]{0:T(1024)}, u32[]{:S(2)}) copy-start(f32[1024]{0:T(1024)} %param.17) | copy-start | bytes 12292
  428.4 1.1 copy-start.8
  428.4 1.2 copy-start.11
  428.4 459.5 %reduce-scatter.11.cloned.1.call-start = ((), (), s32[]{:S(2)}) async-start(), calls=%async_computation.15 | async-start | bytes 11894784 | tf_op jit(solution)/shard_map/reduce_scatter | solution.py:215
  435.5 1.4 copy-start.5
  435.5 945.6 %reduce-scatter.9.cloned.1.call-start = ((), (), s32[]{:S(2)}) async-start(), calls=%async_computation.14 | async-start | bytes 23789568 | tf_op jit(solution)/shard_map/reduce_scatter | solution.py:220
  447.7 1.1 copy-start.9
  453.1 5.1 copy-start.18
  453.1 44.0 %copy-start.7 = (f32[128,1024]{1,0:T(8,128)S(1)}, f32[128,1024]{1,0:T(8,128)}, u32[]{:S(2)}) copy-start(f32[128,1024]{1,0:T(8,128)} %copy-done.6) | copy-start | bytes 1572868
Sparse Core Ops, SparseCore 0:
  10.9 72.2 all-gather.4
  86.1 57.7 all-gather.6
  146.7 90.0 all-gather.8
  239.5 65.6 all-gather.10
  333.4 143.9 reduce-scatter.6
  483.9 153.1 reduce-scatter.4
  640.1 247.7 reduce-scatter.10
  890.9 490.1 reduce-scatter.8
where the time goes:
time: 1390 us
  waiting for transfers between devices  1140 us (82%)
  matrix products  98.6 us (7%)
  blocking collectives  71.7 us (5%)
  local copies, waits for them, and re-layouts  31.8 us (2%)
  other arithmetic  18.2 us (1%)
  between operations  14.6 us (1%)
    reduce_scatter x1, waiting for transfers between devices, on_device(): lax.psum_scatter(column_term(hidden2, grad_gate_up_b), ('seq', 'fsdp'), s...  493 us
    reduce_scatter x1, waiting for transfers between devices, on_device(): lax.psum_scatter(column_term(activation_b, cotangent), ('seq', 'fsdp'), s...  251 us
    reduce_scatter x1, waiting for transfers between devices, on_device(): lax.psum_scatter(column_term(hidden1, grad_projected), ('seq', 'fsdp'), s...  139 us
    all_gather x1, waiting for transfers between devices, on_device(): lax.all_gather(gate_up_weight, ('seq', 'fsdp'), axis=0, tiled=True)  79.5 us
    all_gather x1, waiting for transfers between devices, on_device(): lax.all_gather(qkv_weight, ('seq', 'fsdp'), axis=0, tiled=True)  70.3 us
    all_gather x1, waiting for transfers between devices, on_device(): lax.all_gather(down_weight, ('seq', 'fsdp'), axis=0, tiled=True)  60.7 us
    psum x1, blocking collectives, on_device(): lax.psum((ln1_gain_part, ln1_bias_part, bias_part, ln2_gain_part, ln2_bia...  38.4 us
    all_to_all x1, blocking collectives, on_device(): lax.all_to_all(grad_packed, 'seq', split_axis=0, concat_axis=2, tiled=True)  33.2 us
  transfers between devices with their start and end apart: 11, of which 9 were waited for; matrix products, arithmetic and copies ran while one was open for 9% of the time, Pallas kernels for 0%

commit v1 on v0

--- a/solution.py
+++ b/solution.py
@@ -7,6 +7,13 @@
 HD = 64
 ROT = 16
 EPS = 1e-05
+
+
+def swap_blocks(array, axis, split, join):
+    peers = lax.axis_size(axis)
+    shards = jnp.stack(jnp.split(array, peers, axis=split), axis=0)
+    shards = lax.all_to_all(shards, axis, split_axis=0, concat_axis=0)
+    return jnp.concatenate(shards, axis=join)
 
 
 def layer_norm(values, gain_vec, shift_vec):
@@ -185,7 +192,7 @@
         axis=1,
     )
     packed = packed.reshape(tok_rows, 3, width).astype(jnp.bfloat16)
-    by_heads = lax.all_to_all(packed, "seq", split_axis=2, concat_axis=0, tiled=True)
+    by_heads = swap_blocks(packed, "seq", 2, 0)
     length = by_heads.shape[0]
     local_heads = by_heads.shape[2] // HD
     queries = by_heads[:, 0].reshape(length, local_heads, HD)

time: 1390 us -> 1390 us (level)
  transfers between devices with their start and end apart: 11 -> 11, of which waited for: 9 -> 10; matrix products, arithmetic and copies ran while one was open for 9% -> 9% of each run, Pallas kernels for 0% -> 0%
where the time goes in v1:
time: 1390 us
  waiting for transfers between devices  1140 us (82%)
  matrix products  98.7 us (7%)
  blocking collectives  71.7 us (5%)
  local copies, waits for them, and re-layouts  35.2 us (3%)
  other arithmetic  18.2 us (1%)
  between operations  14.6 us (1%)
    reduce_scatter x1, waiting for transfers between devices, on_device(): lax.psum_scatter(column_term(hidden2, grad_gate_up_b), ('seq', 'fsdp'), s...  493 us
    reduce_scatter x1, waiting for transfers between devices, on_device(): lax.psum_scatter(column_term(activation_b, cotangent), ('seq', 'fsdp'), s...  251 us
    reduce_scatter x1, waiting for transfers between devices, on_device(): lax.psum_scatter(column_term(hidden1, grad_projected), ('seq', 'fsdp'), s...  139 us
    all_gather x1, waiting for transfers between devices, on_device(): lax.all_gather(gate_up_weight, ('seq', 'fsdp'), axis=0, tiled=True)  81.1 us
    all_gather x1, waiting for transfers between devices, on_device(): lax.all_gather(qkv_weight, ('seq', 'fsdp'), axis=0, tiled=True)  70.4 us
    all_gather x1, waiting for transfers between devices, on_device(): lax.all_gather(down_weight, ('seq', 'fsdp'), axis=0, tiled=True)  60.7 us
    psum x1, blocking collectives, on_device(): lax.psum((ln1_gain_part, ln1_bias_part, bias_part, ln2_gain_part, ln2_bia...  38.5 us
    all_to_all x1, blocking collectives, on_device(): lax.all_to_all(grad_packed, 'seq', split_axis=0, concat_axis=2, tiled=True)  33.2 us
  transfers between devices with their start and end apart: 11, of which 10 were waited for; matrix products, arithmetic and copies ran while one was open for 9% of the time, Pallas kernels for 0%

profile of v1, /device:TPU:0, one launch (start us, length us, event | category | flops | bytes accessed | tf_op | source)
XLA Modules:
  0.0 1386.7 jit_solution(16244670282660402855)
XLA Ops:
  11.1 1.2 fusion.59
  12.9 70.4 %all-gather.5.cloned.1.call-done = bf16[1024,3072]{1,0:T(8,128)(2,1)} async-done(((bf16[32,3072]{1,0:T(8,128)(2,1)}), bf16[1024,3072]{1,0:T(8,128)(2,1)}) %all-gather.5.cloned.1.call-update) | async-done | bytes 6291472 | tf_op jit(solution)/shard_map/all_gather | solution.py:182
  83.2 3.9 convolution_add_fusion
  93.1 3.5 all-to-all-start
  96.7 23.6 %all-to-all-done = bf16[8,128,3,128]{1,3,2,0:T(8,128)(2,1)S(1)} async-done(((bf16[8,128,3,128]{1,3,2,0:T(8,128)(2,1)}), bf16[8,128,3,128]{1,3,2,0:T(8,128)(2,1)S(1)}, u32[]{:S(2)}, u32[]{:S(2)}) %all-to-all-start) | async-done | bytes 786464 | tf_op jit(solution)/shard_map/all_to_all | solution.py:15
  123.0 14.4 %while.28 = (s32[]{:T(128)}, bf16[2,512,2,64]{1,3,2,0:T(8,128)(2,1)S(1)}, f32[2,2,512]{2,1,0:T(2,128)S(1)}, s32[2]{0:T(128)S(1)}, bf16[2,512,2,64]{1,3,2,0:T(8,1...) while((s32[]{:T(128)}, ...), condition=%wide.region_5.6_spmd.clone, body=%wide.region_2.5_spmd.clone.sunk | while | flops 281542144 | bytes 15634553 | solution.py:107
  124.6 2.0 fusion.147
  127.8 2.4 fusion.149
  131.9 2.0 fusion.147
  135.0 2.4 fusion.149
  138.7 3.6 all-to-all-start.1
  142.4 9.4 all-to-all-done.1
  151.8 2.3 fusion.102
  154.4 81.1 %all-gather.9.cloned.1.call-done = bf16[1024,5632]{1,0:T(8,128)(2,1)} async-done(((bf16[32,5632]{1,0:T(8,128)(2,1)}), bf16[1024,5632]{1,0:T(8,128)(2,1)}) %all-gather.9.cloned.1.call-update) | async-done | bytes 11534352 | tf_op jit(solution)/shard_map/all_gather | solution.py:206
  235.5 7.7 fusion.98
  243.2 60.7 %all-gather.11.cloned.1.call-done = bf16[2816,1024]{1,0:T(8,128)(2,1)} async-done(((bf16[88,1024]{1,0:T(8,128)(2,1)}), bf16[2816,1024]{1,0:T(8,128)(2,1)}) %all-gather.11.cloned.1.call-update) | async-done | bytes 5767184 | tf_op jit(solution)/shard_map/all_gather | solution.py:207
  303.9 7.7 fusion.84
  311.6 6.6 multiply_reduce_fusion.1
  318.2 1.3 fusion.100
  321.4 1.5 convolution_convert_fusion
  323.0 1.8 copy.80
  324.7 3.6 all-to-all-start.2
  328.4 3.6 fusion.103
  332.5 5.6 all-to-all-done.2
  339.1 42.1 %while.29 = (s32[]{:T(128)}, f32[1024,2,64]{0,2,1:T(8,128)}, f32[1024,2,64]{0,2,1:T(8,128)}, f32[2,512,2,64]{1,0,3,2:T(2,128)}, bf16[2,512,2,64]{1,3,2,0:T(8,128...) while((s32[]{:T(128)}, f32[1024,2,64]{0,2,1:T(8,128)}, ...), condition=%wide.region_12.13_spmd.clone, body=%wide.region_10.12_spmd.clone.sunk | while | flops 688061952 | bytes 55083208 | solution.py:156
  339.1 1.6 fusion.159
  342.5 2.8 multiply_reduce_fusion.5
  345.3 1.3 multiply_convert_fusion.3
  346.6 2.2 fusion.160
  348.8 4.4 fusion.161
  354.2 5.7 dynamic_update_slice.21
  360.0 1.6 fusion.159
  363.4 2.8 multiply_reduce_fusion.5
  366.2 1.3 multiply_convert_fusion.3
  367.5 2.4 fusion.160
  369.9 4.5 fusion.161
  375.5 5.7 dynamic_update_slice.21
  383.3 1.5 reshape.368
  386.7 33.2 %all_to_all.52 = bf16[1024,3,128]{2,1,0:T(4,128)(2,1)S(1)} all-to-all(bf16[1024,3,128]{2,1,0:T(4,128)(2,1)S(1)} %copy.77), channel_id=1, replica_groups=mesh['seq'=8,'fsdp'=4] {'seq'}, dimensions={0} | all-to-all | bytes 1572864 | tf_op jit(solution)/shard_map/all_to_all | solution.py:252
  420.6 6.5 fusion.67
  428.2 5.9 fusion.70
  435.5 10.9 fusion.82
  447.5 4.3 fusion.48
  451.8 5.1 fusion.99
  457.3 38.5 %all-reduce.2 = (f32[1024]{0:T(1024)}, f32[1024]{0:T(1024)}, f32[3072]{0:T(1024)}, f32[1024]{0:T(1024)}, f32[1024]{0:T(1024)}) all-reduce(f32[1024]{0:T(1024)S(1)} %get-tuple-element.239, f32[1024]{0:T(1024)S(1)} %get-tuple-element.242, f32[3072]{0:T(1024)S(1)} %bitcast.236, ...), channel_id=1, replica_groups=mesh['seq'=8,'fsdp'=4] {'seq','fsdp'}, use_global_device_ids=true, to_apply=%region_16.17 | all-reduce | flops 7168 | bytes 57344 | tf_op jit(solution)/shard_map/psum | solution.py:261
  496.9 139.1 %reduce-scatter.5.cloned.1.call-done = f32[32,3072]{1,0:T(8,128)} async-done(((f32[1024,3072]{1,0:T(8,128)}), f32[32,3072]{1,0:T(8,128)}) %reduce-scatter.5.cloned.1.call-update) | async-done | bytes 393232 | tf_op jit(solution)/shard_map/reduce_scatter | solution.py:254
  636.0 250.8 %reduce-scatter.11.cloned.1.call-done = f32[88,1024]{1,0:T(8,128)} async-done(((f32[2816,1024]{1,0:T(8,128)}), f32[88,1024]{1,0:T(8,128)}) %reduce-scatter.11.cloned.1.call-update) | async-done | bytes 360464 | tf_op jit(solution)/shard_map/reduce_scatter | solution.py:222
  886.8 493.0 %reduce-scatter.9.cloned.1.call-done = f32[32,5632]{1,0:T(8,128)} async-done(((f32[1024,5632]{1,0:T(8,128)}), f32[32,5632]{1,0:T(8,128)}) %reduce-scatter.9.cloned.1.call-update) | async-done | bytes 720912 | tf_op jit(solution)/shard_map/reduce_scatter | solution.py:227
  (142 shorter events, 38.6 us)
Async XLA Ops:
  7.2 76.0 %all-gather.5.cloned.1.call-start = ((), (), s32[]{:S(2)}) async-start(), calls=%async_computation.8 | async-start | bytes 6488064 | tf_op jit(solution)/shard_map/all_gather | solution.py:182
  7.9 134.5 %all-gather.7.cloned.1.call-start = ((), (), s32[]{:S(2)}) async-start(), calls=%async_computation.9 | async-start | bytes 2162688 | tf_op jit(solution)/shard_map/all_gather | solution.py:183
  8.7 226.8 %all-gather.9.cloned.1.call-start = ((), (), s32[]{:S(2)}) async-start(), calls=%async_computation.10 | async-start | bytes 11894784 | tf_op jit(solution)/shard_map/all_gather | solution.py:206
  9.4 294.5 %all-gather.11.cloned.1.call-start = ((), (), s32[]{:S(2)}) async-start(), calls=%async_computation.11 | async-start | bytes 5947392 | tf_op jit(solution)/shard_map/all_gather | solution.py:207
  12.2 0.5 copy-start.17
  93.1 27.2 %all-to-all-start = ((bf16[8,128,3,128]{1,3,2,0:T(8,128)(2,1)}), bf16[8,128,3,128]{1,3,2,0:T(8,128)(2,1)S(1)}, u32[]{:S(2)}, u32[]{:S(2)}) async-start(bf16[8,128,3,128]{1,3,2,0:T(8,128)(2,1)} %fusion.85), calls=%async_computation | async-start | bytes 1572864 | tf_op jit(solution)/shard_map/all_to_all | solution.py:15
  123.0 28.7 %copy-start.2 = (bf16[1,128,1024]{2,1,0:T(8,128)(2,1)S(1)}, bf16[1,128,1024]{2,1,0:T(8,128)(2,1)}, u32[]{:S(2)}) copy-start(bf16[1,128,1024]{2,1,0:T(8,128)(2,1)} %param.15) | copy-start | bytes 786436
  137.5 98.0 %copy-start.13 = (f32[1024]{0:T(1024)S(1)}, f32[1024]{0:T(1024)}, u32[]{:S(2)}) copy-start(f32[1024]{0:T(1024)} %param.21) | copy-start | bytes 12292
  137.5 98.0 %copy-start.15 = (f32[1024]{0:T(1024)S(1)}, f32[1024]{0:T(1024)}, u32[]{:S(2)}) copy-start(f32[1024]{0:T(1024)} %param.22) | copy-start | bytes 12292
  138.7 13.1 all-to-all-start.1
  151.8 2.6 copy-start.12
  154.4 149.6 %copy-start.10 = (bf16[1,128,1024]{2,1,0:T(8,128)(2,1)S(1)}, bf16[1,128,1024]{2,1,0:T(8,128)(2,1)}, u32[]{:S(2)}) copy-start(bf16[1,128,1024]{2,1,0:T(8,128)(2,1)} %param.25) | copy-start | bytes 786436
  303.9 7.7 copy-start.1
  311.6 9.8 copy-start.4
  319.5 0.8 copy-start.6
  324.7 13.3 all-to-all-start.2
  328.3 168.6 %reduce-scatter.7.cloned.1.call-start = ((), (), s32[]{:S(2)}) async-start(), calls=%async_computation.13 | async-start | bytes 4325376 | tf_op jit(solution)/shard_map/reduce_scatter | solution.py:238
  332.0 304.0 %reduce-scatter.5.cloned.1.call-start = ((), (), s32[]{:S(2)}) async-start(), calls=%async_computation.12 | async-start | bytes 12976128 | tf_op jit(solution)/shard_map/reduce_scatter | solution.py:254
  340.7 4.5 copy-start
  361.6 4.5 copy-start
  385.8 34.7 %copy-start.3 = (bf16[1,128,1024]{2,1,0:T(8,128)(2,1)S(1)}, bf16[1,128,1024]{2,1,0:T(8,128)(2,1)}, u32[]{:S(2)}) copy-start(bf16[1,128,1024]{2,1,0:T(8,128)(2,1)} %param.15) | copy-start | bytes 786436
  385.9 34.7 %copy-start.14 = (f32[1024]{0:T(1024)S(1)}, f32[1024]{0:T(1024)}, u32[]{:S(2)}) copy-start(f32[1024]{0:T(1024)} %param.16) | copy-start | bytes 12292
  385.9 34.7 %copy-start.16 = (f32[1024]{0:T(1024)S(1)}, f32[1024]{0:T(1024)}, u32[]{:S(2)}) copy-start(f32[1024]{0:T(1024)} %param.17) | copy-start | bytes 12292
  427.1 1.1 copy-start.8
  427.1 1.2 copy-start.11
  427.1 459.7 %reduce-scatter.11.cloned.1.call-start = ((), (), s32[]{:S(2)}) async-start(), calls=%async_computation.15 | async-start | bytes 11894784 | tf_op jit(solution)/shard_map/reduce_scatter | solution.py:222
  434.1 1.4 copy-start.5
  434.2 945.7 %reduce-scatter.9.cloned.1.call-start = ((), (), s32[]{:S(2)}) async-start(), calls=%async_computation.14 | async-start | bytes 23789568 | tf_op jit(solution)/shard_map/reduce_scatter | solution.py:227
  446.4 1.1 copy-start.9
  451.8 5.1 copy-start.18
  451.8 44.0 %copy-start.7 = (f32[128,1024]{1,0:T(8,128)S(1)}, f32[128,1024]{1,0:T(8,128)}, u32[]{:S(2)}) copy-start(f32[128,1024]{1,0:T(8,128)} %copy-done.6) | copy-start | bytes 1572868
Sparse Core Ops, SparseCore 0:
  10.9 72.2 all-gather.4
  86.1 56.2 all-gather.6
  145.3 90.1 all-gather.8
  238.2 65.6 all-gather.10
  332.1 143.7 reduce-scatter.6
  482.4 153.5 reduce-scatter.4
  639.0 247.7 reduce-scatter.10
  889.8 490.0 reduce-scatter.8
